TPU v7x, 32 devices: a whole 2x2x4 slice. The times are simulated.
32 devices in a mesh: dp: 8 (over y, x, core), expert: 4 (over z).
Axes of the slice: x: 2, y: 2, z: 4, core: 2. Of those that a mesh axis runs over, the one named last changes fastest.
Arguments:
- tokens: bfloat16 [4096, 2048], P(('dp', 'expert')), may hold values from -6 to 6
- routes: int32 [4096, 2], P(('dp', 'expert')), may hold values from 0 to 3, all different within a row; in each aligned block of 128 rows (0 to 127, 128 to 255, ...) at most 80 rows name the same one
- gates: float32 [4096, 2], P(('dp', 'expert')), may hold values from 0.2 to 1
- cotangent: bfloat16 [4096, 2048], P(('dp', 'expert')), may hold values from -6 to 6
- w_gate: bfloat16 [4, 2048, 384], P('expert', 'dp'), may hold values from -0.125 to 0.125
- w_up: bfloat16 [4, 2048, 384], P('expert', 'dp'), may hold values from -0.125 to 0.125
- w_down: bfloat16 [4, 384, 2048], P('expert', None, 'dp'), may hold values from -0.3125 to 0.3125
Outputs:
- mixed: bfloat16 [4096, 2048], P(('dp', 'expert'))
- token_grads: bfloat16 [4096, 2048], P(('dp', 'expert'))
- gate_grads: float32 [4096, 2], P(('dp', 'expert'))
- grad_gate: float32 [4, 2048, 384], P('expert', 'dp')
- grad_up: float32 [4, 2048, 384], P('expert', 'dp')
- grad_down: float32 [4, 384, 2048], P('expert', None, 'dp')
Inputs may be any that keep to these rules, and one draw needn't show every extreme that they name: `routes`: each row names 2 different experts. Within the 128 rows of one device no expert is named by more than 80 rows, a bound that some expert reaches in some device's rows.
All inputs are finite; a program needn't handle non-finite values.
Results may differ from a plain program's by a relative error of at most 0.015.
Values may be sent and summed in bfloat16 or wider, within the bound.
A program may use at most 64 MiB of HBM per device.

v0:
```python
import jax
import jax.numpy as jnp
from jax import lax
from jax.sharding import PartitionSpec as P


def contract_last(left, right):
    return lax.dot_general(
        left, right, (((1,), (1,)), ((), ())), preferred_element_type=jnp.float32
    )


def contract_first(left, right):
    return lax.dot_general(
        left, right, (((0,), (0,)), ((), ())), preferred_element_type=jnp.float32
    )


def body(tokens, routes, gates, cotangent, w_gate, w_up, w_down):
    experts = lax.axis_size("expert")
    token_rows = tokens.shape[0]
    picks = routes.shape[1]
    width = tokens.shape[1]
    capacity = max(2, 5 * token_rows * picks // (4 * experts))
    entries = token_rows * picks
    slot_count = experts * capacity
    flat_routes = routes.reshape(entries)
    member = (flat_routes[:, None] == jnp.arange(experts, dtype=jnp.int32)[None, :]).astype(
        jnp.int32
    )
    earlier = jnp.cumsum(member, axis=0) - member
    target = flat_routes * capacity + jnp.sum(earlier * member, axis=1)
    placing = (jnp.arange(slot_count, dtype=jnp.int32)[:, None] == target[None, :]).astype(
        jnp.bfloat16
    )
    placing_tokens = jnp.sum(placing.reshape(slot_count, token_rows, picks), axis=2)
    outbound = jnp.dot(placing_tokens, tokens, preferred_element_type=jnp.float32).astype(
        jnp.bfloat16
    )
    outbound = outbound.reshape(experts, capacity, width)
    scaled = (gates[:, :, None] * cotangent.astype(jnp.float32)[:, None, :]).astype(jnp.bfloat16)
    grad_outbound = jnp.dot(
        placing, scaled.reshape(entries, width), preferred_element_type=jnp.float32
    )
    grad_outbound = grad_outbound.astype(jnp.bfloat16).reshape(experts, capacity, width)
    inbound = lax.all_to_all(outbound, "expert", split_axis=0, concat_axis=0, tiled=True)
    slot_rows = inbound.reshape(slot_count, width)
    full_gate, full_up, full_down = (
        lax.all_gather(w_gate, "dp", axis=1, tiled=True),
        lax.all_gather(w_up, "dp", axis=1, tiled=True),
        lax.all_gather(w_down, "dp", axis=2, tiled=True),
    )
    full_gate = full_gate[0]
    full_up = full_up[0]
    full_down = full_down[0]
    gate_pre = jnp.dot(slot_rows, full_gate, preferred_element_type=jnp.float32)
    up_pre = jnp.dot(slot_rows, full_up, preferred_element_type=jnp.float32)
    sigma = jax.nn.sigmoid(gate_pre)
    swish = gate_pre * sigma
    hidden = (swish * up_pre).astype(jnp.bfloat16)
    expert_out = jnp.dot(hidden, full_down, preferred_element_type=jnp.float32).astype(jnp.bfloat16)
    returned = lax.all_to_all(
        expert_out.reshape(experts, capacity, width),
        "expert",
        split_axis=0,
        concat_axis=0,
        tiled=True,
    )
    per_entry = contract_first(placing, returned.reshape(slot_count, width)).reshape(
        token_rows, picks, width
    )
    mixed = jnp.sum(gates[:, :, None] * per_entry, axis=1).astype(jnp.bfloat16)
    gate_grads = jnp.sum(cotangent.astype(jnp.float32)[:, None, :] * per_entry, axis=2)
    grad_inbound = lax.all_to_all(grad_outbound, "expert", split_axis=0, concat_axis=0, tiled=True)
    grad_rows = grad_inbound.reshape(slot_count, width)
    d_hidden = contract_last(grad_rows, full_down)
    d_gate = (d_hidden * up_pre * sigma * (1.0 + gate_pre * (1.0 - sigma))).astype(jnp.bfloat16)
    d_up = (d_hidden * swish).astype(jnp.bfloat16)
    part_gate = contract_first(slot_rows, d_gate)
    part_up = contract_first(slot_rows, d_up)
    part_down = contract_first(hidden, grad_rows)
    shares = (
        lax.psum_scatter(
            part_gate.astype(jnp.bfloat16), "dp", scatter_dimension=0, tiled=True
        ).astype(jnp.float32),
        lax.psum_scatter(
            part_up.astype(jnp.bfloat16), "dp", scatter_dimension=0, tiled=True
        ).astype(jnp.float32),
        lax.psum_scatter(
            part_down.astype(jnp.bfloat16), "dp", scatter_dimension=1, tiled=True
        ).astype(jnp.float32),
    )
    entry_grad = (contract_last(d_gate, full_gate) + contract_last(d_up, full_up)).astype(
        jnp.bfloat16
    )
    arrived = lax.all_to_all(
        entry_grad.reshape(experts, capacity, width),
        "expert",
        split_axis=0,
        concat_axis=0,
        tiled=True,
    )
    token_grads = contract_first(placing_tokens, arrived.reshape(slot_count, width)).astype(
        jnp.bfloat16
    )
    return (mixed, token_grads, gate_grads, shares[0][None], shares[1][None], shares[2][None])


def solution(mesh):
    return jax.shard_map(
        body,
        mesh=mesh,
        in_specs=(
            P(("dp", "expert"), None),
            P(("dp", "expert"), None),
            P(("dp", "expert"), None),
            P(("dp", "expert"), None),
            P("expert", "dp", None),
            P("expert", "dp", None),
            P("expert", None, "dp"),
        ),
        out_specs=(
            P(("dp", "expert"), None),
            P(("dp", "expert"), None),
            P(("dp", "expert"), None),
            P("expert", "dp", None),
            P("expert", "dp", None),
            P("expert", None, "dp"),
        ),
        check_vma=False,
    )
```

profile of v0, /device:TPU:0, one launch (start us, length us, event | category | flops | bytes accessed | tf_op | source)
XLA Modules:
  0.0 229.6 jit_solution(18241620535647696961)
XLA Ops:
  7.2 0.0 copy-start
  7.2 0.0 all-gather.4.cloned.1.call-start
  7.2 0.7 all-gather.4.cloned.1.call-update
  7.9 0.0 all-gather.6.cloned.1.call-start
  8.0 0.7 all-gather.6.cloned.1.call-update
  8.7 0.8 copy.35
  9.5 0.1 eq.62
  9.6 0.1 reshape.105
  9.7 1.2 reduce-window.6
  11.0 0.1 slice.8
  11.0 0.1 copy.37
  11.2 0.1 copy.38
  11.3 0.1 add_bitcast_fusion
  11.4 0.1 reduce_sum.42
  11.5 0.1 copy.39
  11.6 0.7 multiply_add_fusion
  12.3 0.0 copy-done
  12.4 1.6 convolution_convert_fusion.3
  13.9 6.5 %all-to-all-start = ((bf16[4,80,2048]{2,1,0:T(8,128)(2,1)}), bf16[4,80,2048]{2,1,0:T(8,128)(2,1)}, u32[]{:S(2)}, u32[]{:S(2)}) async-start(bf16[4,80,2048]{2,1,0:T(8,128)(2,1)} %bitcast.2), calls=%async_computation | async-start | bytes 2621440 | tf_op jit(solution)/shard_map/all_to_all | solution.py:46
  20.4 0.7 all-gather.8.cloned.1.call-update
  21.1 0.0 copy-done.1
  21.1 1.0 mul.82.clone
  22.2 0.0 copy-start.5
  22.2 2.5 %mul.83 = f32[256,2048]{1,0:T(8,128)} reshape(f32[128,2,2048]{2,1,0:T(2,128)S(1)} %mul.82.clone) | data formatting | bytes 4194304 | tf_op jit(solution)/shard_map/mul | solution.py:41
  24.6 0.1 copy.41
  24.8 0.1 mul.80
  24.9 3.2 %convolution_convert_fusion.4 = bf16[320,2048]{1,0:T(8,128)(2,1)} fusion(f32[256,2048]{1,0:T(8,128)} %mul.83, f32[256]{0:T(256)S(1)} %mul.80, s32[256]{0:T(256)S(1)} %multiply_add_fusion.1), kind=kOutput, calls=%fused_computation.6 | convolution fusion | flops 337330176 | bytes 3409920 | tf_op jit(solution)/shard_map/dot_general | solution.py:42
  28.2 23.7 %all-to-all-done = bf16[4,80,2048]{2,1,0:T(8,128)(2,1)} async-done(((bf16[4,80,2048]{2,1,0:T(8,128)(2,1)}), bf16[4,80,2048]{2,1,0:T(8,128)(2,1)}, u32[]{:S(2)}, u32[]{:S(2)}) %all-to-all-start) | async-done | bytes 1310752 | tf_op jit(solution)/shard_map/all_to_all | solution.py:46
  51.9 3.5 %all-to-all-start.2 = ((bf16[4,80,2048]{2,1,0:T(8,128)(2,1)}), bf16[4,80,2048]{2,1,0:T(8,128)(2,1)S(1)}, u32[]{:S(2)}, u32[]{:S(2)}) async-start(bf16[4,80,2048]{2,1,0:T(8,128)(2,1)} %bitcast.10), calls=%async_computation.2 | async-start | bytes 2621440 | tf_op jit(solution)/shard_map/all_to_all | solution.py:74
  55.4 0.0 reduce-scatter.4.cloned.1.call-start
  55.4 0.0 all-gather.4.cloned.1.call-done
  55.5 2.7 %fusion.9 = f32[320,384]{1,0:T(8,128)S(1)} fusion(bf16[320,2048]{1,0:T(8,128)(2,1)} %bitcast.3, bf16[1,2048,384]{2,1,0:T(8,128)(2,1)} %all-gather.4.cloned.1.call-done), kind=kOutput, calls=%fused_computation.20 | convolution fusion | flops 503316480 | bytes 3375104 | tf_op jit(solution)/shard_map/dot_general | solution.py:56
  58.1 7.6 %all-gather.6.cloned.1.call-done = bf16[1,2048,384]{2,1,0:T(8,128)(2,1)} async-done(((bf16[1,256,384]{2,1,0:T(8,128)(2,1)}), bf16[1,2048,384]{2,1,0:T(8,128)(2,1)}) %all-gather.6.cloned.1.call-update) | async-done | bytes 1572880 | tf_op jit(solution)/shard_map/all_gather | solution.py:50
  65.7 3.4 %fusion.5 = f32[320,384]{1,0:T(8,128)} fusion(bf16[320,2048]{1,0:T(8,128)(2,1)} %bitcast.3, bf16[1,2048,384]{2,1,0:T(8,128)(2,1)} %all-gather.6.cloned.1.call-done), kind=kOutput, calls=%fused_computation.16 | convolution fusion | flops 503316480 | bytes 3375104 | tf_op jit(solution)/shard_map/dot_general | solution.py:57
  69.2 17.1 %all-to-all-done.2 = bf16[4,80,2048]{2,1,0:T(8,128)(2,1)S(1)} async-done(((bf16[4,80,2048]{2,1,0:T(8,128)(2,1)}), bf16[4,80,2048]{2,1,0:T(8,128)(2,1)S(1)}, u32[]{:S(2)}, u32[]{:S(2)}) %all-to-all-start.2) | async-done | bytes 1310752 | tf_op jit(solution)/shard_map/all_to_all | solution.py:74
  86.3 7.2 %all-gather.8.cloned.1.call-done = bf16[1,384,2048]{2,1,0:T(8,128)(2,1)} async-done(((bf16[1,384,256]{2,1,0:T(8,128)(2,1)}), bf16[1,384,2048]{2,1,0:T(8,128)(2,1)}) %all-gather.8.cloned.1.call-update) | async-done | bytes 1572880 | tf_op jit(solution)/shard_map/all_gather | solution.py:51
  93.4 2.5 %multiply_convert_fusion.2 = (bf16[320,384]{1,0:T(8,128)(2,1)S(1)}, bf16[320,384]{1,0:T(8,128)(2,1)S(1)}, bf16[320,384]{1,0:T(8,128)(2,1)S(1)}) fusion(f32[320,384]{1,0:T(8,128)S(1)} %fusion.9, f32[320,384]{1,0:T(8,128)} %fusion.5, bf16[320,2048]{1,0:T(8,128)(2,1)S(1)} %bitcast.72, bf16[1,384,2048]{2,1,0:T(8,128)(2,1)} %all-gather.8.cloned.1.call-done), kind=kOutput, calls=%fused_computation.23 | convolution fusion | flops 505159680 | bytes 4603904 | tf_op jit(solution)/shard_map/dot_general | solution.py:8
  95.9 3.6 %convolution_convert_fusion.2 = bf16[2048,384]{1,0:T(8,128)(2,1)} fusion(bf16[320,2048]{1,0:T(8,128)(2,1)} %bitcast.3, bf16[320,384]{1,0:T(8,128)(2,1)S(1)} %get-tuple-element.9), kind=kOutput, calls=%fused_computation.3 | convolution fusion | flops 504102912 | bytes 3129344 | tf_op jit(solution)/shard_map/dot_general | solution.py:14
  99.5 0.0 reduce-scatter.4.cloned.1.call-update
  99.5 0.0 reduce-scatter.6.cloned.1.call-start
  99.6 3.6 %convolution_convert_fusion.1 = bf16[2048,384]{1,0:T(8,128)(2,1)} fusion(bf16[320,2048]{1,0:T(8,128)(2,1)} %bitcast.3, bf16[320,384]{1,0:T(8,128)(2,1)S(1)} %get-tuple-element.8), kind=kOutput, calls=%fused_computation.2 | convolution fusion | flops 504102912 | bytes 3129344 | tf_op jit(solution)/shard_map/dot_general | solution.py:14
  103.2 0.0 reduce-scatter.6.cloned.1.call-update
  103.3 0.0 copy-start.3
  103.3 2.4 %fusion.7 = f32[320,2048]{1,0:T(8,128)S(1)} fusion(bf16[320,384]{1,0:T(8,128)(2,1)S(1)} %get-tuple-element.9, bf16[1,2048,384]{2,1,0:T(8,128)(2,1)} %all-gather.4.cloned.1.call-done), kind=kOutput, calls=%fused_computation.18 | convolution fusion | flops 503316480 | bytes 4440064 | tf_op jit(solution)/shard_map/dot_general | solution.py:8
  105.7 0.0 copy-done.3
  105.7 2.0 fusion
  107.7 4.6 %all-to-all-start.3 = ((bf16[4,80,2048]{2,1,0:T(8,128)(2,1)}), bf16[4,80,2048]{2,1,0:T(8,128)(2,1)S(1)}, u32[]{:S(2)}, u32[]{:S(2)}) async-start(bf16[4,80,2048]{2,1,0:T(8,128)(2,1)} %bitcast.75), calls=%async_computation.3 | async-start | bytes 2621440 | tf_op jit(solution)/shard_map/all_to_all | solution.py:96
  112.3 3.4 %convolution_convert_fusion.5 = bf16[320,2048]{1,0:T(8,128)(2,1)} fusion(bf16[320,384]{1,0:T(8,128)(2,1)S(1)} %get-tuple-element.10, bf16[1,384,2048]{2,1,0:T(8,128)(2,1)} %all-gather.8.cloned.1.call-done), kind=kOutput, calls=%fused_computation.7 | convolution fusion | flops 503971840 | bytes 3129344 | tf_op jit(solution)/shard_map/dot_general | solution.py:61
  115.6 28.4 %all-to-all-done.3 = bf16[4,80,2048]{2,1,0:T(8,128)(2,1)S(1)} async-done(((bf16[4,80,2048]{2,1,0:T(8,128)(2,1)}), bf16[4,80,2048]{2,1,0:T(8,128)(2,1)S(1)}, u32[]{:S(2)}, u32[]{:S(2)}) %all-to-all-start.3) | async-done | bytes 1310752 | tf_op jit(solution)/shard_map/all_to_all | solution.py:96
  144.0 4.3 %all-to-all-start.1 = ((bf16[4,80,2048]{2,1,0:T(8,128)(2,1)}), bf16[4,80,2048]{2,1,0:T(8,128)(2,1)}, u32[]{:S(2)}, u32[]{:S(2)}) async-start(bf16[4,80,2048]{2,1,0:T(8,128)(2,1)} %bitcast.7), calls=%async_computation.1 | async-start | bytes 2621440 | tf_op jit(solution)/shard_map/all_to_all | solution.py:62
  148.4 0.2 reduce-scatter.8.cloned.1.call-start
  148.6 2.2 convolution_convert_fusion
  150.8 0.0 reduce-scatter.8.cloned.1.call-update
  150.8 1.0 copy-done.2
  151.8 1.2 convert_element_type.67
  153.0 0.1 iota_compare_fusion
  153.1 0.1 eq.68
  153.3 1.3 convolution_convert_fusion.6
  154.6 24.8 %all-to-all-done.1 = bf16[4,80,2048]{2,1,0:T(8,128)(2,1)} async-done(((bf16[4,80,2048]{2,1,0:T(8,128)(2,1)}), bf16[4,80,2048]{2,1,0:T(8,128)(2,1)}, u32[]{:S(2)}, u32[]{:S(2)}) %all-to-all-start.1) | async-done | bytes 1310752 | tf_op jit(solution)/shard_map/all_to_all | solution.py:62
  179.3 3.1 %multiply_reduce_fusion = (f32[128,2]{0,1:T(2,128)}, bf16[128,2048]{1,0:T(8,128)(2,1)}) fusion(f32[128,2048]{1,0:T(8,128)S(1)} %copy-done.4, f32[128,2]{0,1:T(2,128)S(1)} %copy-done.5, bf16[320,2048,1]{1,0,2:T(8,128)(2,1)} %bitcast.9, pred[128,2,320]{2,1,0:T(4,128)(4,1)S(1)} %eq.68), kind=kOutput, calls=%fused_computation.9 | convolution fusion | flops 337379072 | bytes 2967552 | tf_op jit(solution)/shard_map/dot_general | solution.py:14
  182.4 1.7 bitcast_convert_fusion.2
  184.1 1.7 bitcast_convert_fusion.1
  185.8 35.2 %reduce-scatter.8.cloned.1.call-done = bf16[384,256]{1,0:T(8,128)(2,1)} async-done(((bf16[384,2048]{1,0:T(8,128)(2,1)}), bf16[384,256]{1,0:T(8,128)(2,1)}) %reduce-scatter.8.cloned.1.call-update) | async-done | bytes 196624 | tf_op jit(solution)/shard_map/reduce_scatter | solution.py:89
  221.1 1.7 bitcast_convert_fusion
  (14 shorter events, 0.1 us)
Async XLA Ops:
  7.2 5.2 %copy-start = (bf16[128,2048]{1,0:T(8,128)(2,1)S(1)}, bf16[128,2048]{1,0:T(8,128)(2,1)}, u32[]{:S(2)}) copy-start(bf16[128,2048]{1,0:T(8,128)(2,1)} %param.7) | copy-start | bytes 1572868
  7.2 48.3 %all-gather.4.cloned.1.call-start = ((), (), s32[]{:S(2)}) async-start(), calls=%async_computation.7 | async-start | bytes 1769472 | tf_op jit(solution)/shard_map/all_gather | solution.py:49
  7.9 57.8 %all-gather.6.cloned.1.call-start = ((), (), s32[]{:S(2)}) async-start(), calls=%async_computation.8 | async-start | bytes 1769472 | tf_op jit(solution)/shard_map/all_gather | solution.py:50
  13.9 7.2 %copy-start.1 = (bf16[128,2048]{1,0:T(8,128)(2,1)S(1)}, bf16[128,2048]{1,0:T(8,128)(2,1)}, u32[]{:S(2)}) copy-start(bf16[128,2048]{1,0:T(8,128)(2,1)} %param.10) | copy-start | bytes 1572868
  13.9 37.9 %all-to-all-start = ((bf16[4,80,2048]{2,1,0:T(8,128)(2,1)}), bf16[4,80,2048]{2,1,0:T(8,128)(2,1)}, u32[]{:S(2)}, u32[]{:S(2)}) async-start(bf16[4,80,2048]{2,1,0:T(8,128)(2,1)} %bitcast.2), calls=%async_computation | async-start | bytes 2621440 | tf_op jit(solution)/shard_map/all_to_all | solution.py:46
  20.4 73.0 %all-gather.8.cloned.1.call-start = ((), (), s32[]{:S(2)}) async-start(), calls=%async_computation.9 | async-start | bytes 1769472 | tf_op jit(solution)/shard_map/all_gather | solution.py:51
  22.2 2.5 %copy-start.5 = (f32[128,2]{0,1:T(2,128)S(1)}, f32[128,2]{0,1:T(2,128)}, u32[]{:S(2)}) copy-start(f32[128,2]{0,1:T(2,128)} %param.9) | copy-start | bytes 3076
  51.9 34.4 %all-to-all-start.2 = ((bf16[4,80,2048]{2,1,0:T(8,128)(2,1)}), bf16[4,80,2048]{2,1,0:T(8,128)(2,1)S(1)}, u32[]{:S(2)}, u32[]{:S(2)}) async-start(bf16[4,80,2048]{2,1,0:T(8,128)(2,1)} %bitcast.10), calls=%async_computation.2 | async-start | bytes 2621440 | tf_op jit(solution)/shard_map/all_to_all | solution.py:74
  55.4 127.0 %reduce-scatter.4.cloned.1.call-start = ((), (), s32[]{:S(2)}) async-start(), calls=%async_computation.10 | async-start | bytes 1769472 | tf_op jit(solution)/shard_map/reduce_scatter | solution.py:83
  99.5 84.6 %reduce-scatter.6.cloned.1.call-start = ((), (), s32[]{:S(2)}) async-start(), calls=%async_computation.11 | async-start | bytes 1769472 | tf_op jit(solution)/shard_map/reduce_scatter | solution.py:86
  103.3 2.4 %copy-start.3 = (bf16[1,2048,384]{2,1,0:T(8,128)(2,1)S(1)}, bf16[1,2048,384]{2,1,0:T(8,128)(2,1)}, u32[]{:S(2)}) copy-start(bf16[1,2048,384]{2,1,0:T(8,128)(2,1)} %all-gather.6.cloned.1.call-done) | copy-start | bytes 4718596
  107.7 36.4 %all-to-all-start.3 = ((bf16[4,80,2048]{2,1,0:T(8,128)(2,1)}), bf16[4,80,2048]{2,1,0:T(8,128)(2,1)S(1)}, u32[]{:S(2)}, u32[]{:S(2)}) async-start(bf16[4,80,2048]{2,1,0:T(8,128)(2,1)} %bitcast.75), calls=%async_computation.3 | async-start | bytes 2621440 | tf_op jit(solution)/shard_map/all_to_all | solution.py:96
  144.0 35.3 %all-to-all-start.1 = ((bf16[4,80,2048]{2,1,0:T(8,128)(2,1)}), bf16[4,80,2048]{2,1,0:T(8,128)(2,1)}, u32[]{:S(2)}, u32[]{:S(2)}) async-start(bf16[4,80,2048]{2,1,0:T(8,128)(2,1)} %bitcast.7), calls=%async_computation.1 | async-start | bytes 2621440 | tf_op jit(solution)/shard_map/all_to_all | solution.py:62
  148.4 72.7 %reduce-scatter.8.cloned.1.call-start = ((), (), s32[]{:S(2)}) async-start(), calls=%async_computation.12 | async-start | bytes 1769472 | tf_op jit(solution)/shard_map/reduce_scatter | solution.py:89
  150.8 1.1 copy-start.2
  153.0 26.3 %copy-start.4 = (f32[128,2048]{1,0:T(8,128)S(1)}, f32[128,2048]{1,0:T(8,128)}, u32[]{:S(2)}) copy-start(f32[128,2048]{1,0:T(8,128)} %convert_element_type.67) | copy-start | bytes 3145732
Sparse Core Ops, SparseCore 0:
  9.9 28.3 all-gather.3
  40.1 25.5 all-gather.5
  67.6 25.7 all-gather.7
  99.7 38.3 reduce-scatter.3
  141.2 38.3 reduce-scatter.5
  182.7 38.3 reduce-scatter.7
where the time goes:
time: 230 us
  waiting for transfers between devices  146 us (63%)
  matrix products  34.9 us (15%)
  starting transfers between devices  19.3 us (8%)
  between operations  14.3 us (6%)
  other arithmetic  8.5 us (4%)
  local copies, waits for them, and re-layouts  6.49 us (3%)
    reduce_scatter x1, waiting for transfers between devices, body(): lax.psum_scatter(part_down.astype(jnp.bfloat16), 'dp', scatter_dimension=...  35.2 us
    all_to_all x1, waiting for transfers between devices, body(): lax.all_to_all(entry_grad.reshape(experts, capacity, width), 'expert', sp...  28.4 us
    all_to_all x1, waiting for transfers between devices, body(): lax.all_to_all(expert_out.reshape(experts, capacity, width), 'expert', sp...  24.8 us
    all_to_all x1, waiting for transfers between devices, body(): lax.all_to_all(outbound, 'expert', split_axis=0, concat_axis=0, tiled=True)  23.7 us
    all_to_all x1, waiting for transfers between devices, body(): lax.all_to_all(grad_outbound, 'expert', split_axis=0, concat_axis=0, tile...  17.1 us
    dot_general x5, matrix products, contract_first(): lax.dot_general(left, right, (((0,), (0,)), ((), ())), preferred_element_...  13.9 us
    all_gather x1, waiting for transfers between devices, body(): lax.all_gather(w_up, 'dp', axis=1, tiled=True)  7.58 us
    all_gather x1, waiting for transfers between devices, body(): lax.all_gather(w_down, 'dp', axis=2, tiled=True)  7.16 us
  transfers between devices with their start and end apart: 10, of which 7 were waited for; matrix products, arithmetic and copies ran while one was open for 18% of the time, Pallas kernels for 0%

commit v1 on v0

--- a/solution.py
+++ b/solution.py
@@ -1,7 +1,29 @@
+import functools
 import jax
 import jax.numpy as jnp
 from jax import lax
 from jax.sharding import PartitionSpec as P
+
+
+def drive_lots_all(u, mesh_dim):
+    top, local_now = (jax.lax.axis_size(mesh_dim), jax.lax.axis_index(mesh_dim))
+    x_next = u.shape[0] // top
+    seen_now = list(u.shape)
+    seen_now[0] = x_next
+    t_next = seen_now[0]
+    seen_now[0] = t_next * top
+    u_next = jnp.zeros(seen_now, u.dtype)
+    for b in range(top):
+        b_next = lax.dynamic_slice_in_dim(u, (local_now ^ b) * x_next, x_next, axis=0)
+        if b:
+            b_next = jax.lax.ppermute(
+                b_next, mesh_dim, list(map(lambda jj: (jj, jj ^ b), range(top)))
+            )
+        u_next = lax.dynamic_update_slice_in_dim(u_next, b_next, (local_now ^ b) * t_next, axis=0)
+    return u_next
+
+
+define_ticks_on = functools.partial(drive_lots_all, mesh_dim="expert")
 
 
 def contract_last(left, right):
@@ -71,7 +93,7 @@
     )
     mixed = jnp.sum(gates[:, :, None] * per_entry, axis=1).astype(jnp.bfloat16)
     gate_grads = jnp.sum(cotangent.astype(jnp.float32)[:, None, :] * per_entry, axis=2)
-    grad_inbound = lax.all_to_all(grad_outbound, "expert", split_axis=0, concat_axis=0, tiled=True)
+    grad_inbound = define_ticks_on(grad_outbound)
     grad_rows = grad_inbound.reshape(slot_count, width)
     d_hidden = contract_last(grad_rows, full_down)
     d_gate = (d_hidden * up_pre * sigma * (1.0 + gate_pre * (1.0 - sigma))).astype(jnp.bfloat16)

time: 230 us -> 229 us (level)
    ppermute x0 -> x3, waiting for transfers between devices: none -> 42.6 us  [drive_lots_all(): jax.lax.ppermute(b_next, mesh_dim, list(map(lambda jj: (jj, jj ^ b), rang...]
    reduce_scatter x1, waiting for transfers between devices: 35.2 us -> 0.01 us  [body(): lax.psum_scatter(part_down.astype(jnp.bfloat16), 'dp', scatter_dimension=...]
    reduce_scatter x1, waiting for transfers between devices: 0.01 us -> 34.4 us  [body(): lax.psum_scatter(part_gate.astype(jnp.bfloat16), 'dp', scatter_dimension=...]
    all_to_all x1, waiting for transfers between devices: 23.7 us -> 0.01 us  [body(): lax.all_to_all(outbound, 'expert', split_axis=0, concat_axis=0, tiled=True)]
    all_to_all x1 -> x0, waiting for transfers between devices: 17.1 us -> none  [body(): lax.all_to_all(grad_outbound, 'expert', split_axis=0, concat_axis=0, tile...]
    all_gather x1, waiting for transfers between devices: 7.58 us -> 0.02 us  [body(): lax.all_gather(w_up, 'dp', axis=1, tiled=True)]
    all_gather x1, waiting for transfers between devices: 7.16 us -> 11.9 us  [body(): lax.all_gather(w_down, 'dp', axis=2, tiled=True)]
    ppermute x0 -> x3, starting transfers between devices: none -> 4.53 us  [drive_lots_all(): jax.lax.ppermute(b_next, mesh_dim, list(map(lambda jj: (jj, jj ^ b), rang...]
  transfers between devices with their start and end apart: 10 -> 12, of which waited for: 7 -> 6; matrix products, arithmetic and copies ran while one was open for 18% -> 18% of each run, Pallas kernels for 0% -> 0%
where the time goes in v1:
time: 229 us; the launch traced here: 228 us
  waiting for transfers between devices  144 us (63%)
  matrix products  33.7 us (15%)
  starting transfers between devices  20.4 us (9%)
  between operations  14.3 us (6%)
  other arithmetic  8.42 us (4%)
  local copies, waits for them, and re-layouts  7.75 us (3%)
    ppermute x3, waiting for transfers between devices, drive_lots_all(): jax.lax.ppermute(b_next, mesh_dim, list(map(lambda jj: (jj, jj ^ b), rang...  42.6 us
    reduce_scatter x1, waiting for transfers between devices, body(): lax.psum_scatter(part_gate.astype(jnp.bfloat16), 'dp', scatter_dimension=...  34.4 us
    all_to_all x1, waiting for transfers between devices, body(): lax.all_to_all(entry_grad.reshape(experts, capacity, width), 'expert', sp...  28.4 us
    all_to_all x1, waiting for transfers between devices, body(): lax.all_to_all(expert_out.reshape(experts, capacity, width), 'expert', sp...  24.3 us
    dot_general x5, matrix products, contract_first(): lax.dot_general(left, right, (((0,), (0,)), ((), ())), preferred_element_...  14.2 us
    all_gather x1, waiting for transfers between devices, body(): lax.all_gather(w_down, 'dp', axis=2, tiled=True)  11.9 us
    all_to_all x1, starting transfers between devices, body(): lax.all_to_all(outbound, 'expert', split_axis=0, concat_axis=0, tiled=True)  6.48 us
    dot_general x3, matrix products, contract_last(): lax.dot_general(left, right, (((1,), (1,)), ((), ())), preferred_element_...  5.53 us
  transfers between devices with their start and end apart: 12, of which 6 were waited for; matrix products, arithmetic and copies ran while one was open for 18% of the time, Pallas kernels for 0%

profile of v1, /device:TPU:0, one launch (start us, length us, event | category | flops | bytes accessed | tf_op | source)
XLA Modules:
  0.0 228.3 jit_solution(6371304609010237357)
XLA Ops:
  7.2 0.0 copy-start
  7.2 0.0 all-gather.6.cloned.1.call-start
  7.2 0.7 all-gather.6.cloned.1.call-update
  7.9 0.0 all-gather.4.cloned.1.call-start
  8.0 0.7 all-gather.4.cloned.1.call-update
  8.7 0.0 all-gather.8.cloned.1.call-start
  8.7 0.7 all-gather.8.cloned.1.call-update
  9.4 0.8 copy.35
  10.2 0.1 eq.62
  10.3 0.1 reshape.105
  10.5 1.2 reduce-window.6
  11.7 0.1 slice.8
  11.8 0.1 copy.37
  11.9 0.1 copy.38
  12.0 0.1 add_bitcast_fusion
  12.1 0.1 reduce_sum.42
  12.3 0.1 copy.39
  12.3 0.7 multiply_add_fusion
  13.1 1.6 convolution_convert_fusion.3
  14.7 6.5 %all-to-all-start = ((bf16[4,80,2048]{2,1,0:T(8,128)(2,1)}), bf16[4,80,2048]{2,1,0:T(8,128)(2,1)}, u32[]{:S(2)}, u32[]{:S(2)}) async-start(bf16[4,80,2048]{2,1,0:T(8,128)(2,1)} %bitcast.2), calls=%async_computation | async-start | bytes 2621440 | tf_op jit(solution)/shard_map/all_to_all | solution.py:68
  21.1 1.0 mul.82.clone
  22.2 0.0 copy-start.4
  22.2 2.5 %mul.83 = f32[256,2048]{1,0:T(8,128)} reshape(f32[128,2,2048]{2,1,0:T(2,128)S(1)} %mul.82.clone) | data formatting | bytes 4194304 | tf_op jit(solution)/shard_map/mul | solution.py:63
  24.7 0.1 copy.41
  24.8 0.1 mul.80
  24.9 2.2 convolution_convert_fusion.4
  27.1 0.1 broadcast_in_dim.28
  27.3 0.1 constant_dynamic-slice_fusion.2
  27.4 2.1 collective-permute-start
  29.5 2.4 %collective-permute-start.1 = (bf16[1,80,2048]{2,1,0:T(8,128)(2,1)S(1)}, bf16[1,80,2048]{2,1,0:T(8,128)(2,1)S(1)}, u32[]{:S(2)}, u32[]{:S(2)}) collective-permute-start(bf16[1,80,2048]{2,1,0:T(8,128)(2,1)S(1)} %get-tuple-element.9), channel_id=1, source_target_pairs={{0,2},{1,3},{2,0},{3,1},{4,6},{5,7},{6,4},{7,5},{8,10},{9,11},{10,... | collective-permute-start | bytes 983048 | tf_op jit(solution)/shard_map/ppermute | solution.py:19
  31.9 0.1 collective-permute-start.2
  31.9 18.6 %collective-permute-done = bf16[1,80,2048]{2,1,0:T(8,128)(2,1)S(1)} collective-permute-done((bf16[1,80,2048]{2,1,0:T(8,128)(2,1)S(1)}, bf16[1,80,2048]{2,1,0:T(8,128)(2,1)S(1)}, u32[]{:S(2)}, u32[]{:S(2)}) %collective-permute-start) | collective-permute-done | bytes 327712 | tf_op jit(solution)/shard_map/ppermute | solution.py:19
  50.6 23.9 %collective-permute-done.1 = bf16[1,80,2048]{2,1,0:T(8,128)(2,1)S(1)} collective-permute-done((bf16[1,80,2048]{2,1,0:T(8,128)(2,1)S(1)}, bf16[1,80,2048]{2,1,0:T(8,128)(2,1)S(1)}, u32[]{:S(2)}, u32[]{:S(2)}) %collective-permute-start.1) | collective-permute-done | bytes 327712 | tf_op jit(solution)/shard_map/ppermute | solution.py:19
  74.6 0.0 all-gather.6.cloned.1.call-done
  74.7 3.5 %fusion.5 = f32[320,384]{1,0:T(8,128)} fusion(bf16[320,2048]{1,0:T(8,128)(2,1)} %bitcast.3, bf16[1,2048,384]{2,1,0:T(8,128)(2,1)} %all-gather.6.cloned.1.call-done), kind=kOutput, calls=%fused_computation.16 | convolution fusion | flops 503316480 | bytes 3375104 | tf_op jit(solution)/shard_map/dot_general | solution.py:79
  78.2 3.4 %fusion.9 = f32[320,384]{1,0:T(8,128)} fusion(bf16[320,2048]{1,0:T(8,128)(2,1)} %bitcast.3, bf16[1,2048,384]{2,1,0:T(8,128)(2,1)} %all-gather.4.cloned.1.call-done), kind=kOutput, calls=%fused_computation.20 | convolution fusion | flops 503316480 | bytes 3375104 | tf_op jit(solution)/shard_map/dot_general | solution.py:78
  81.6 11.9 %all-gather.8.cloned.1.call-done = bf16[1,384,2048]{2,1,0:T(8,128)(2,1)} async-done(((bf16[1,384,256]{2,1,0:T(8,128)(2,1)}), bf16[1,384,2048]{2,1,0:T(8,128)(2,1)}) %all-gather.8.cloned.1.call-update) | async-done | bytes 1572880 | tf_op jit(solution)/shard_map/all_gather | solution.py:73
  93.4 2.6 %multiply_convert_fusion.2 = (bf16[320,384]{1,0:T(8,128)(2,1)S(1)}, bf16[320,384]{1,0:T(8,128)(2,1)S(1)}, bf16[320,384]{1,0:T(8,128)(2,1)S(1)}) fusion(f32[320,384]{1,0:T(8,128)} %fusion.9, f32[320,384]{1,0:T(8,128)} %fusion.5, bf16[320,2048]{1,0:T(8,128)(2,1)S(1)} %bitcast.74, bf16[1,384,2048]{2,1,0:T(8,128)(2,1)} %all-gather.8.cloned.1.call-done), kind=kOutput, calls=%fused_computation.23 | convolution fusion | flops 505159680 | bytes 4603904 | tf_op jit(solution)/shard_map/dot_general | solution.py:30
  96.1 2.2 convolution_convert_fusion
  98.2 0.0 reduce-scatter.8.cloned.1.call-update
  98.2 0.0 reduce-scatter.6.cloned.1.call-start
  98.3 3.6 %convolution_convert_fusion.1 = bf16[2048,384]{1,0:T(8,128)(2,1)} fusion(bf16[320,2048]{1,0:T(8,128)(2,1)} %bitcast.3, bf16[320,384]{1,0:T(8,128)(2,1)S(1)} %get-tuple-element.12), kind=kOutput, calls=%fused_computation.2 | convolution fusion | flops 504102912 | bytes 3129344 | tf_op jit(solution)/shard_map/dot_general | solution.py:36
  101.9 0.0 reduce-scatter.6.cloned.1.call-update
  102.0 1.4 copy-done.3
  103.3 0.9 fusion.7
  104.2 0.6 copy-done.2
  104.8 2.1 fusion
  106.8 4.7 %all-to-all-start.2 = ((bf16[4,80,2048]{2,1,0:T(8,128)(2,1)}), bf16[4,80,2048]{2,1,0:T(8,128)(2,1)S(1)}, u32[]{:S(2)}, u32[]{:S(2)}) async-start(bf16[4,80,2048]{2,1,0:T(8,128)(2,1)} %bitcast.12), calls=%async_computation.2 | async-start | bytes 2621440 | tf_op jit(solution)/shard_map/all_to_all | solution.py:118
  111.5 3.3 %convolution_convert_fusion.5 = bf16[320,2048]{1,0:T(8,128)(2,1)} fusion(bf16[320,384]{1,0:T(8,128)(2,1)S(1)} %get-tuple-element.14, bf16[1,384,2048]{2,1,0:T(8,128)(2,1)} %all-gather.8.cloned.1.call-done), kind=kOutput, calls=%fused_computation.7 | convolution fusion | flops 503971840 | bytes 3129344 | tf_op jit(solution)/shard_map/dot_general | solution.py:83
  114.8 28.4 %all-to-all-done.2 = bf16[4,80,2048]{2,1,0:T(8,128)(2,1)S(1)} async-done(((bf16[4,80,2048]{2,1,0:T(8,128)(2,1)}), bf16[4,80,2048]{2,1,0:T(8,128)(2,1)S(1)}, u32[]{:S(2)}, u32[]{:S(2)}) %all-to-all-start.2) | async-done | bytes 1310752 | tf_op jit(solution)/shard_map/all_to_all | solution.py:118
  143.2 4.3 %all-to-all-start.1 = ((bf16[4,80,2048]{2,1,0:T(8,128)(2,1)}), bf16[4,80,2048]{2,1,0:T(8,128)(2,1)}, u32[]{:S(2)}, u32[]{:S(2)}) async-start(bf16[4,80,2048]{2,1,0:T(8,128)(2,1)} %bitcast.7), calls=%async_computation.1 | async-start | bytes 2621440 | tf_op jit(solution)/shard_map/all_to_all | solution.py:84
  147.6 0.2 reduce-scatter.4.cloned.1.call-start
  147.8 3.7 %convolution_convert_fusion.2 = bf16[2048,384]{1,0:T(8,128)(2,1)} fusion(bf16[320,2048]{1,0:T(8,128)(2,1)} %bitcast.3, bf16[320,384]{1,0:T(8,128)(2,1)S(1)} %get-tuple-element.13), kind=kOutput, calls=%fused_computation.3 | convolution fusion | flops 504102912 | bytes 3129344 | tf_op jit(solution)/shard_map/dot_general | solution.py:36
  151.5 0.0 reduce-scatter.4.cloned.1.call-update
  151.6 1.1 convert_element_type.67
  152.6 0.1 iota_compare_fusion
  152.8 0.1 eq.68
  152.9 1.3 convolution_convert_fusion.6
  154.2 24.3 %all-to-all-done.1 = bf16[4,80,2048]{2,1,0:T(8,128)(2,1)} async-done(((bf16[4,80,2048]{2,1,0:T(8,128)(2,1)}), bf16[4,80,2048]{2,1,0:T(8,128)(2,1)}, u32[]{:S(2)}, u32[]{:S(2)}) %all-to-all-start.1) | async-done | bytes 1310752 | tf_op jit(solution)/shard_map/all_to_all | solution.py:84
  178.5 3.4 %multiply_reduce_fusion = (f32[128,2]{0,1:T(2,128)}, bf16[128,2048]{1,0:T(8,128)(2,1)}) fusion(f32[128,2048]{1,0:T(8,128)} %convert_element_type.67, f32[128,2]{0,1:T(2,128)S(1)} %copy-done.4, bf16[320,2048,1]{1,0,2:T(8,128)(2,1)} %bitcast.9, pred[128,2,320]{2,1,0:T(4,128)(4,1)S(1)} %eq.68), kind=kOutput, calls=%fused_computation.9 | convolution fusion | flops 337379072 | bytes 2967552 | tf_op jit(solution)/shard_map/dot_general | solution.py:36
  181.9 1.7 bitcast_convert_fusion
  183.6 1.7 bitcast_convert_fusion.1
  185.3 34.4 %reduce-scatter.4.cloned.1.call-done = bf16[256,384]{1,0:T(8,128)(2,1)} async-done(((bf16[2048,384]{1,0:T(8,128)(2,1)}), bf16[256,384]{1,0:T(8,128)(2,1)}) %reduce-scatter.4.cloned.1.call-update) | async-done | bytes 196624 | tf_op jit(solution)/shard_map/reduce_scatter | solution.py:105
  219.8 1.7 bitcast_convert_fusion.2
  (21 shorter events, 0.2 us)
Async XLA Ops:
  7.2 5.9 %copy-start = (bf16[128,2048]{1,0:T(8,128)(2,1)S(1)}, bf16[128,2048]{1,0:T(8,128)(2,1)}, u32[]{:S(2)}) copy-start(bf16[128,2048]{1,0:T(8,128)(2,1)} %param.7) | copy-start | bytes 1572868
  7.2 67.5 %all-gather.6.cloned.1.call-start = ((), (), s32[]{:S(2)}) async-start(), calls=%async_computation.7 | async-start | bytes 1769472 | tf_op jit(solution)/shard_map/all_gather | solution.py:72
  7.9 70.2 %all-gather.4.cloned.1.call-start = ((), (), s32[]{:S(2)}) async-start(), calls=%async_computation.6 | async-start | bytes 1769472 | tf_op jit(solution)/shard_map/all_gather | solution.py:71
  8.7 84.8 %all-gather.8.cloned.1.call-start = ((), (), s32[]{:S(2)}) async-start(), calls=%async_computation.8 | async-start | bytes 1769472 | tf_op jit(solution)/shard_map/all_gather | solution.py:73
  14.7 6.5 %copy-start.1 = (bf16[128,2048]{1,0:T(8,128)(2,1)S(1)}, bf16[128,2048]{1,0:T(8,128)(2,1)}, u32[]{:S(2)}) copy-start(bf16[128,2048]{1,0:T(8,128)(2,1)} %param.10) | copy-start | bytes 1572868
  14.7 60.0 %all-to-all-start = ((bf16[4,80,2048]{2,1,0:T(8,128)(2,1)}), bf16[4,80,2048]{2,1,0:T(8,128)(2,1)}, u32[]{:S(2)}, u32[]{:S(2)}) async-start(bf16[4,80,2048]{2,1,0:T(8,128)(2,1)} %bitcast.2), calls=%async_computation | async-start | bytes 2621440 | tf_op jit(solution)/shard_map/all_to_all | solution.py:68
  21.1 160.8 %reduce-scatter.8.cloned.1.call-start = ((), (), s32[]{:S(2)}) async-start(), calls=%async_computation.11 | async-start | bytes 1769472 | tf_op jit(solution)/shard_map/reduce_scatter | solution.py:111
  22.2 2.5 %copy-start.4 = (f32[128,2]{0,1:T(2,128)S(1)}, f32[128,2]{0,1:T(2,128)}, u32[]{:S(2)}) copy-start(f32[128,2]{0,1:T(2,128)} %param.9) | copy-start | bytes 3076
  27.4 23.1 %collective-permute-start = (bf16[1,80,2048]{2,1,0:T(8,128)(2,1)S(1)}, bf16[1,80,2048]{2,1,0:T(8,128)(2,1)S(1)}, u32[]{:S(2)}, u32[]{:S(2)}) collective-permute-start(bf16[1,80,2048]{2,1,0:T(8,128)(2,1)S(1)} %get-tuple-element.10), channel_id=1, source_target_pairs={{0,1},{1,0},{2,3},{3,2},{4,5},{5,4},{6,7},{7,6},{8,9},{9,8},{10,11... | collective-permute-start | bytes 983048 | tf_op jit(solution)/shard_map/ppermute | solution.py:19
  29.5 45.0 %collective-permute-start.1 = (bf16[1,80,2048]{2,1,0:T(8,128)(2,1)S(1)}, bf16[1,80,2048]{2,1,0:T(8,128)(2,1)S(1)}, u32[]{:S(2)}, u32[]{:S(2)}) collective-permute-start(bf16[1,80,2048]{2,1,0:T(8,128)(2,1)S(1)} %get-tuple-element.9), channel_id=1, source_target_pairs={{0,2},{1,3},{2,0},{3,1},{4,6},{5,7},{6,4},{7,5},{8,10},{9,11},{10,... | collective-permute-start | bytes 983048 | tf_op jit(solution)/shard_map/ppermute | solution.py:19
  31.9 42.7 %collective-permute-start.2 = (bf16[1,80,2048]{2,1,0:T(8,128)(2,1)S(1)}, bf16[1,80,2048]{2,1,0:T(8,128)(2,1)S(1)}, u32[]{:S(2)}, u32[]{:S(2)}) collective-permute-start(bf16[1,80,2048]{2,1,0:T(8,128)(2,1)S(1)} %get-tuple-element.8), channel_id=1, source_target_pairs={{0,3},{1,2},{2,1},{3,0},{4,7},{5,6},{6,5},{7,4},{8,11},{9,10},{10,... | collective-permute-start | bytes 983048 | tf_op jit(solution)/shard_map/ppermute | solution.py:19
  98.2 85.4 %reduce-scatter.6.cloned.1.call-start = ((), (), s32[]{:S(2)}) async-start(), calls=%async_computation.10 | async-start | bytes 1769472 | tf_op jit(solution)/shard_map/reduce_scatter | solution.py:108
  101.9 1.4 copy-start.3
  103.3 1.4 copy-start.2
  106.8 36.4 %all-to-all-start.2 = ((bf16[4,80,2048]{2,1,0:T(8,128)(2,1)}), bf16[4,80,2048]{2,1,0:T(8,128)(2,1)S(1)}, u32[]{:S(2)}, u32[]{:S(2)}) async-start(bf16[4,80,2048]{2,1,0:T(8,128)(2,1)} %bitcast.12), calls=%async_computation.2 | async-start | bytes 2621440 | tf_op jit(solution)/shard_map/all_to_all | solution.py:118
  143.2 35.3 %all-to-all-start.1 = ((bf16[4,80,2048]{2,1,0:T(8,128)(2,1)}), bf16[4,80,2048]{2,1,0:T(8,128)(2,1)}, u32[]{:S(2)}, u32[]{:S(2)}) async-start(bf16[4,80,2048]{2,1,0:T(8,128)(2,1)} %bitcast.7), calls=%async_computation.1 | async-start | bytes 2621440 | tf_op jit(solution)/shard_map/all_to_all | solution.py:84
  147.6 72.2 %reduce-scatter.4.cloned.1.call-start = ((), (), s32[]{:S(2)}) async-start(), calls=%async_computation.9 | async-start | bytes 1769472 | tf_op jit(solution)/shard_map/reduce_scatter | solution.py:105
Sparse Core Ops, SparseCore 0:
  9.9 28.3 all-gather.5
  40.1 25.5 all-gather.3
  67.6 25.7 all-gather.7
  98.4 38.3 reduce-scatter.7
  139.9 38.3 reduce-scatter.5
  181.4 38.3 reduce-scatter.3
